TPU v7x, 256 devices: a whole 4x4x8 slice. The times are simulated.
256 devices in a mesh: pole: 4 (over y), row: 8 (over z_lo, x), col: 8 (over z_hi, core).
Axes of the slice: x: 4, y: 4, z: 8 (z_hi: 4, z_lo: 2; z = z_hi * 2 + z_lo), core: 2. Of those that a mesh axis runs over, the one named last changes fastest.
Arguments:
- found_inverse: bfloat16 [4, 2, 8192, 8, 8, 128], P('pole', None, 'row', None, 'col'), may hold values from -0.125 to 0.125
- l_panel: bfloat16 [4, 2, 8192, 512], P('pole', None, ('row', 'col')), may hold values from -1.5 to 1.5
- block_pattern: int32 [64, 4], P(('row', 'col')), may hold values 0 or 1
- sup_widths: int32 [4], replicated, may hold values from 1 to 128, 320 in all
- diag_inverse: bfloat16 [4, 2, 512, 128], P('pole'), may hold values from -6 to 6
- pole_weights: float32 [4, 2], P('pole'), may hold values from -4 to 4
Outputs:
- density: float32 [512, 8192], P('col', 'row')
- diagonal: float32 [512, 128], replicated
Inputs may be any that keep to these rules, and one draw needn't show every extreme that they name: `sup_widths`: one supernode has exactly 128 columns.
All inputs are finite; a program needn't handle non-finite values. No bound on the sum of `block_pattern` on one device may be relied on, other than what follows from the above.
Results may differ from a plain program's by a relative error of at most 0.0003.
Values may be sent and summed in bfloat16 or wider, within the bound.
A program may use at most 128 MiB of HBM per device.

v0:
```python
import jax
import jax.numpy as jnp
from jax import lax
from jax.sharding import PartitionSpec as P


def contract(left, right):
    return jnp.einsum("jk,ij->ki", left, right, preferred_element_type=jnp.float32)


def pair_product(left, right):
    return jnp.einsum("ika,kbi->kab", left, right, precision=lax.Precision.HIGHEST)


def per_device(found_inverse, l_panel, block_pattern, sup_widths, diag_inverse, pole_weights):
    slot_width = diag_inverse.shape[-1]
    total_cols = l_panel.shape[-1]
    supernodes = total_cols // slot_width
    row_count = lax.axis_size("row")
    col_count = lax.axis_size("col")
    row_index = lax.axis_index("row")
    col_index = lax.axis_index("col")
    columns = jnp.arange(total_cols, dtype=jnp.int32)
    column_ok = columns % slot_width < jnp.repeat(sup_widths, slot_width)
    block_ok = jnp.repeat(block_pattern[0], slot_width) == 1
    masked = jnp.where(
        (column_ok & block_ok)[None, None, :], l_panel[0], jnp.zeros((), jnp.bfloat16)
    )
    everything = lax.all_gather(masked, ("row", "col"), axis=1, tiled=True)
    own_rows = lax.dynamic_slice_in_dim(
        everything, row_index * col_count * slot_width, col_count * slot_width, 1
    )
    grouped = everything.reshape(2, row_count, col_count, slot_width, total_cols)
    picked = lax.dynamic_index_in_dim(grouped, col_index, 2, keepdims=False)
    column_rows = picked.reshape(2, row_count * slot_width, total_cols)
    local_rows = found_inverse.shape[2]
    inverse = found_inverse[0].reshape(2, local_rows, row_count * slot_width)
    part_real = contract(column_rows[1], inverse[1]) - contract(column_rows[0], inverse[0])
    part_imag = -(contract(column_rows[1], inverse[0]) + contract(column_rows[0], inverse[1]))
    w_real = pole_weights[0, 0]
    w_imag = pole_weights[0, 1]
    weighted = w_real * part_real - w_imag * part_imag
    whole = lax.psum(weighted, "pole")
    density = lax.psum_scatter(whole, "col", scatter_dimension=0, tiled=True)
    lifted = own_rows.astype(jnp.float32).reshape(2, local_rows, supernodes, slot_width)
    upper_real = part_real.reshape(supernodes, slot_width, local_rows)
    upper_imag = part_imag.reshape(supernodes, slot_width, local_rows)
    t_real = pair_product(lifted[0], upper_real) - pair_product(lifted[1], upper_imag)
    t_imag = pair_product(lifted[0], upper_imag) + pair_product(lifted[1], upper_real)
    lead_flag = ((row_index == 0) & (col_index == 0)).astype(jnp.float32)
    d_real = diag_inverse[0, 0].astype(jnp.float32).reshape(supernodes, slot_width, slot_width)
    d_imag = diag_inverse[0, 1].astype(jnp.float32).reshape(supernodes, slot_width, slot_width)
    local_term = lead_flag * (w_real * d_real - w_imag * d_imag) - (
        w_real * t_real - w_imag * t_imag
    )
    diagonal = lax.psum(local_term.reshape(total_cols, slot_width), ("pole", "row", "col"))
    return (density, diagonal)


def solution(mesh):
    in_specs = (
        P("pole", None, "row", None, "col", None),
        P("pole", None, ("row", "col"), None),
        P(("row", "col"), None),
        P(),
        P("pole", None, None, None),
        P("pole", None),
    )
    out_specs = (P("col", "row"), P())
    return jax.shard_map(
        per_device, mesh=mesh, in_specs=in_specs, out_specs=out_specs, check_vma=False
    )
```

profile of v0, /device:TPU:2, one launch (start us, length us, event | category | flops | bytes accessed | tf_op | source)
XLA Modules:
  0.0 514.2 jit_solution(14721515015720495059)
XLA Ops:
  7.2 0.0 all-gather.2.cloned.1.call-start
  7.2 0.7 compare_bitcast_fusion
  7.9 0.7 fusion.25
  8.6 1.7 bitcast_select_fusion
  10.3 0.0 all-gather.2.cloned.1.call-update
  10.3 0.0 reduce-scatter.2.cloned.1.call-start
  10.4 1.3 fusion.27
  11.7 3.8 fusion.26
  15.5 127.3 %all-gather.2.cloned.1.call-done = bf16[2,8192,512]{2,1,0:T(8,128)(2,1)} async-done(((bf16[2,128,512]{2,1,0:T(8,128)(2,1)}), bf16[2,8192,512]{2,1,0:T(8,128)(2,1)}) %all-gather.2.cloned.1.call-update) | async-done | bytes 16777232 | tf_op jit(solution)/shard_map/all_gather | solution.py:29
  142.8 1.7 constant_dynamic-slice_fusion.3
  144.6 1.3 fusion
  145.9 1.3 fusion.2
  147.2 0.3 copy-done.2
  147.5 1.3 fusion.12
  148.8 4.6 multiply_subtract_fusion
  153.4 0.0 all-reduce.3.cloned.1.call-start
  153.4 0.9 copy-done.3
  154.3 1.3 subtract_multiply_fusion
  155.6 3.0 constant_dynamic-slice_fusion.2
  158.6 1.5 copy.9
  160.1 2.3 copy.8
  162.3 3.3 fusion.29
  165.7 1.2 fusion.28
  166.9 0.4 copy-done
  167.3 1.9 fusion.20
  169.1 2.5 fusion.19
  171.6 0.0 all-reduce.5.cloned.1.call-start
  171.7 25.0 %reduce-scatter.2.cloned.1.call-done = f32[64,1024]{1,0:T(8,128)} async-done(((f32[512,1024]{1,0:T(8,128)}), f32[64,1024]{1,0:T(8,128)}) %reduce-scatter.2.cloned.1.call-update) | async-done | bytes 262160 | tf_op jit(solution)/shard_map/reduce_scatter | solution.py:44
  196.7 259.6 %all-reduce.3.cloned.1.call-done = f32[512,128]{1,0:T(8,128)} async-done(((f32[512,128]{1,0:T(8,128)}), f32[512,128]{1,0:T(8,128)}) %all-reduce.3.cloned.1.call-update) | async-done | bytes 262160 | tf_op jit(solution)/shard_map/psum | solution.py:56
  456.3 48.0 %all-reduce.5.cloned.1.call-done = f32[64,1024]{1,0:T(8,128)} async-done(((f32[64,1024]{1,0:T(8,128)}), f32[64,1024]{1,0:T(8,128)}) %all-reduce.5.cloned.1.call-update) | async-done | bytes 262160 | tf_op jit(solution)/shard_map/psum | solution.py:43
  504.3 1.7 copy.36
  506.0 1.7 copy.37
  (8 shorter events, 0.1 us)
Async XLA Ops:
  7.2 135.7 %all-gather.2.cloned.1.call-start = ((), (), s32[]{:S(2)}) async-start(), calls=%async_computation.1 | async-start | bytes 17039360 | tf_op jit(solution)/shard_map/all_gather | solution.py:29
  10.3 186.4 %reduce-scatter.2.cloned.1.call-start = ((), (), s32[]{:S(2)}) async-start(), calls=%async_computation.3 | async-start | bytes 2359296 | tf_op jit(solution)/shard_map/reduce_scatter | solution.py:44
  145.9 1.6 copy-start.2
  153.4 0.9 copy-start.3
  153.4 302.9 %all-reduce.3.cloned.1.call-start = ((), (), s32[]{:S(2)}) async-start(), calls=%async_computation.2 | async-start | bytes 524288 | tf_op jit(solution)/shard_map/psum | solution.py:56
  162.3 3.3 copy-start.1
  165.7 1.6 copy-start
  171.6 332.7 %all-reduce.5.cloned.1.call-start = ((), (), s32[]{:S(2)}) async-start(), calls=%async_computation.4 | async-start | bytes 524288 | tf_op jit(solution)/shard_map/psum | solution.py:43
Sparse Core Ops, SparseCore 0:
  10.4 132.3 all-gather.1
  153.5 43.1 reduce-scatter.1
  202.7 253.5 all-reduce.2
  458.5 45.7 all-reduce.4
where the time goes:
time: 515 us; the launch traced here: 514 us
  waiting for transfers between devices  460 us (89%)
  local copies, waits for them, and re-layouts  18.5 us (4%)
  matrix products  17.3 us (3%)
  between operations  13.9 us (3%)
    psum x1, waiting for transfers between devices, per_device(): lax.psum(local_term.reshape(total_cols, slot_width), ('pole', 'row', 'col'))  260 us
    all_gather x1, waiting for transfers between devices, per_device(): everything = lax.all_gather(masked, ('row', 'col'), axis=1, tiled=True)  127 us
    psum x1, waiting for transfers between devices, per_device(): whole = lax.psum(weighted, 'pole')  48 us
    reduce_scatter x1, waiting for transfers between devices, per_device(): density = lax.psum_scatter(whole, 'col', scatter_dimension=0, tiled=True)  25 us
  transfers between devices with their start and end apart: 4, of which 4 were waited for; matrix products, arithmetic and copies ran while one was open for 4% of the time, Pallas kernels for 0%

commit v1 on v0

--- a/solution.py
+++ b/solution.py
@@ -53,7 +53,9 @@
     local_term = lead_flag * (w_real * d_real - w_imag * d_imag) - (
         w_real * t_real - w_imag * t_imag
     )
-    diagonal = lax.psum(local_term.reshape(total_cols, slot_width), ("pole", "row", "col"))
+    diagonal = lax.psum(
+        lax.psum(local_term.reshape(total_cols, slot_width), ("row", "col")), "pole"
+    )
     return (density, diagonal)
 
 

time: 515 us -> 444 us (0.86)
  waiting for transfers between devices: 460 us -> 395 us
    psum x1, waiting for transfers between devices: 260 us -> 174 us  [per_device(): lax.psum(local_term.reshape(total_cols, slot_width), ('row', 'col'))]
    reduce_scatter x1, waiting for transfers between devices: 25 us -> 45.1 us  [per_device(): density = lax.psum_scatter(whole, 'col', scatter_dimension=0, tiled=True)]
  transfers between devices with their start and end apart: 4 -> 4, of which waited for: 4 -> 4; matrix products, arithmetic and copies ran while one was open for 4% -> 2% of each run, Pallas kernels for 0% -> 0%
where the time goes in v1:
time: 444 us
  waiting for transfers between devices  395 us (89%)
  matrix products  14.7 us (3%)
  local copies, waits for them, and re-layouts  14.4 us (3%)
  between operations  13.9 us (3%)
  other arithmetic  5.4 us (1%)
    psum x1, waiting for transfers between devices, per_device(): lax.psum(local_term.reshape(total_cols, slot_width), ('row', 'col'))  174 us
    all_gather x1, waiting for transfers between devices, per_device(): everything = lax.all_gather(masked, ('row', 'col'), axis=1, tiled=True)  124 us
    psum x1, waiting for transfers between devices, per_device(): whole = lax.psum(weighted, 'pole')  50.6 us
    reduce_scatter x1, waiting for transfers between devices, per_device(): density = lax.psum_scatter(whole, 'col', scatter_dimension=0, tiled=True)  45.1 us
  transfers between devices with their start and end apart: 4, of which 4 were waited for; matrix products, arithmetic and copies ran while one was open for 2% of the time, Pallas kernels for 0%

profile of v1, /device:TPU:2, one launch (start us, length us, event | category | flops | bytes accessed | tf_op | source)
XLA Modules:
  0.0 443.8 jit_solution(14336903163932519314)
XLA Ops:
  7.2 0.0 all-gather.2.cloned.1.call-start
  7.2 0.7 compare_bitcast_fusion
  7.9 0.7 fusion.25
  8.6 1.7 bitcast_select_fusion
  10.3 0.0 all-gather.2.cloned.1.call-update
  10.3 0.0 all-reduce.4.cloned.1.call-start
  10.4 1.4 fusion.27
  11.7 2.3 subtract_multiply_fusion
  14.1 4.4 %fusion.26 = (bf16[1,1,1024,8,1,128]{5,3,4,2,1,0:T(8,128)(2,1)}, bf16[1,1,1024,8,1,128]{5,3,4,2,1,0:T(8,128)(2,1)}) fusion(bf16[1,2,1024,8,1,128]{5,3,4,2,1,0:T(8,128)(2,1)} %param.6), kind=kLoop, calls=%fused_computation.35 | loop fusion | bytes 8388608 | tf_op jit(solution)/shard_map/slice | solution.py:38
  18.5 124.3 %all-gather.2.cloned.1.call-done = bf16[2,8192,512]{2,1,0:T(8,128)(2,1)} async-done(((bf16[2,128,512]{2,1,0:T(8,128)(2,1)}), bf16[2,8192,512]{2,1,0:T(8,128)(2,1)}) %all-gather.2.cloned.1.call-update) | async-done | bytes 16777232 | tf_op jit(solution)/shard_map/all_gather | solution.py:29
  142.8 1.7 constant_dynamic-slice_fusion.2
  144.5 0.5 copy.9
  145.0 0.5 copy.8
  145.6 1.9 constant_dynamic-slice_fusion.3
  147.5 0.3 copy-done.1
  147.8 1.3 fusion
  149.1 1.3 fusion.2
  150.4 0.3 copy-done
  150.7 1.3 fusion.12
  152.0 4.1 multiply_subtract_fusion
  156.1 1.2 fusion.29
  157.3 1.2 fusion.28
  158.4 1.8 fusion.20
  160.3 2.6 fusion.19
  162.9 0.0 reduce-scatter.2.cloned.1.call-start
  162.9 0.7 reduce-scatter.2.cloned.1.call-update
  163.6 0.0 all-reduce.6.cloned.1.call-start
  163.7 174.5 %all-reduce.4.cloned.1.call-done = f32[512,128]{1,0:T(8,128)} async-done(((f32[512,128]{1,0:T(8,128)}), f32[512,128]{1,0:T(8,128)}) %all-reduce.4.cloned.1.call-update) | async-done | bytes 262160 | tf_op jit(solution)/shard_map/psum | solution.py:57
  338.2 45.1 %reduce-scatter.2.cloned.1.call-done = f32[64,1024]{1,0:T(8,128)} async-done(((f32[512,1024]{1,0:T(8,128)}), f32[64,1024]{1,0:T(8,128)}) %reduce-scatter.2.cloned.1.call-update) | async-done | bytes 262160 | tf_op jit(solution)/shard_map/reduce_scatter | solution.py:44
  383.3 50.6 %all-reduce.6.cloned.1.call-done = (f32[64,1024]{1,0:T(8,128)}, f32[512,128]{1,0:T(8,128)}) async-done(((f32[64,1024]{1,0:T(8,128)}, f32[512,128]{1,0:T(8,128)}), (f32[64,1024]{1,0:T(8,128)}, f32[512,128]{1,0:T(8,128)})) %all-reduce.6.cloned.1.call-update) | async-done | bytes 524304 | tf_op jit(solution)/shard_map/psum | solution.py:43
  433.9 1.7 copy.37
  435.6 1.7 copy.38
  (4 shorter events, 0.0 us)
Async XLA Ops:
  7.2 135.7 %all-gather.2.cloned.1.call-start = ((), (), s32[]{:S(2)}) async-start(), calls=%async_computation.1 | async-start | bytes 17039360 | tf_op jit(solution)/shard_map/all_gather | solution.py:29
  10.3 327.9 %all-reduce.4.cloned.1.call-start = ((), (), s32[]{:S(2)}) async-start(), calls=%async_computation.2 | async-start | bytes 524288 | tf_op jit(solution)/shard_map/psum | solution.py:57
  145.6 2.2 copy-start.1
  149.1 1.6 copy-start
  162.9 220.4 %reduce-scatter.2.cloned.1.call-start = ((), (), s32[]{:S(2)}) async-start(), calls=%async_computation.3 | async-start | bytes 2359296 | tf_op jit(solution)/shard_map/reduce_scatter | solution.py:44
  163.6 270.3 %all-reduce.6.cloned.1.call-start = ((), (), s32[]{:S(2)}) async-start(), calls=%async_computation.4 | async-start | bytes 1048576 | tf_op jit(solution)/shard_map/psum | solution.py:43
Sparse Core Ops, SparseCore 0:
  10.4 132.3 all-gather.1
  163.0 175.1 all-reduce.3
  340.7 42.5 reduce-scatter.1
  385.6 48.2 all-reduce.5
